TPU v7x, 32 devices: a whole 2x2x4 slice. The times are simulated.
32 devices in a mesh: group: 2 (over y), lender: 4 (over z), tensor: 4 (over x, core).
Axes of the slice: x: 2, y: 2, z: 4, core: 2. Of those that a mesh axis runs over, the one named last changes fastest.
Arguments:
- activations: bfloat16 [16, 8192], P('group', 'lender'), parts along dimension 0, may hold values from -400 to 400
- norm_gain: bfloat16 [8192], P('lender'), may hold values from 0.099609375 to 1.8984375
- w_query: bfloat16 [8192, 8192], P('lender', 'tensor'), may hold values from -0.0625 to 0.0625
- w_out: bfloat16 [8192, 8192], P('tensor', 'lender'), may hold values from -0.0625 to 0.0625
- key_pool: bfloat16 [8, 256, 128, 128], P('tensor', ('group', 'lender')), parts along dimension 1, may hold values from -800 to 800
- value_block_store: bfloat16 [8, 256, 128, 128], P('tensor', ('group', 'lender')), parts along dimension 1, may hold values from -48 to 48
- block_list: int32 [16, 8, 16], P('group', 'tensor'), parts along dimension 0, may hold values from 0 to 127, as said below
- block_slot_table: int32 [8, 256], P('tensor', 'group'), parts along dimension 1, may hold values from 0 to 127, each once within a row
- kept_len: int32 [16, 8], P('group', 'tensor'), parts along dimension 0, may hold values from 1 to 16, as said below
Outputs:
- output: bfloat16 [16, 8192], P(('group', 'tensor'), 'lender'), parts along dimension 0
There are 2 independent parts, one for each index of `group`. A program takes and returns all parts, laid end to end along the dimension named above; an argument that names none is the same for every part. Nothing has to cross between parts.
Inputs may be any that keep to these rules, and one draw needn't show every extreme that they name: `block_list`: for each KV head, no logical block appears twice among all rows' lists. `kept_len`: some row of every KV head keeps 16 blocks and some other row keeps one.
All inputs are finite; a program needn't handle non-finite values.
Results may differ from a plain program's by a relative error of at most 0.012.
The roundings to bfloat16 on the way count: a program that leaves them out, or rounds other values in their place, can miss the bound.
Values may be sent and summed in bfloat16 or wider, within the bound.
No kernel may reach another device: no remote copies, remote signals or barrier semaphores. Data moves between devices by JAX's collectives and lax.ppermute only.
A program may use at most 64 MiB of HBM per device.

v0:
```python
import jax
import jax.numpy as jnp
from jax import lax
from jax.sharding import PartitionSpec as P

D = 8192
very_low = -1e30
epsilon = 1e-05


def per_device(
    activations,
    norm_gain,
    w_query,
    w_out,
    key_pool,
    value_block_store,
    block_list,
    block_slot_table,
    kept_len,
):
    row_count = activations.shape[0]
    kv_heads = key_pool.shape[0]
    slot_count = key_pool.shape[1]
    head_dim = key_pool.shape[3]
    kept_most = block_list.shape[2]
    features = activations.astype(jnp.float32)
    squares = jnp.sum(features * features, axis=1)
    scaled = (features * norm_gain.astype(jnp.float32)).astype(jnp.bfloat16)
    partial_value = jnp.dot(scaled, w_query, preferred_element_type=jnp.float32)
    projected, square_sum = lax.psum((partial_value, squares), "lender")
    inverse = lax.rsqrt(square_sum / D + epsilon)
    query_vectors = (projected * inverse[:, None] * head_dim ** (-0.5)).astype(jnp.bfloat16)
    group_size = query_vectors.shape[1] // (kv_heads * head_dim)
    query_vectors = query_vectors.reshape(row_count, kv_heads, group_size, head_dim)
    slot_lookup_table = jnp.broadcast_to(
        block_slot_table[None], (row_count,) + block_slot_table.shape
    )
    slot_ids = jnp.take_along_axis(slot_lookup_table, block_list, axis=2)
    positions = jnp.arange(kept_most, dtype=jnp.int32)
    is_live = positions[None, None, :] < kept_len[:, :, None]
    local_slot = slot_ids - lax.axis_index("lender") * slot_count
    matches = is_live[..., None] & (
        local_slot[..., None] == jnp.arange(slot_count, dtype=jnp.int32)
    )
    owner_mask = jnp.transpose(jnp.any(matches, axis=2), (1, 2, 0))
    owner_half = owner_mask.astype(jnp.bfloat16)
    owner_full = owner_mask.astype(jnp.float32)
    used_slot = jnp.any(owner_mask, axis=2)
    picked = jnp.einsum(
        "hsr,rhgd->hsgd", owner_half, query_vectors, preferred_element_type=jnp.float32
    ).astype(jnp.bfloat16)
    scores = jnp.einsum("hsgd,hstd->hsgt", picked, key_pool, preferred_element_type=jnp.float32)
    block_best = jnp.max(scores, axis=3)
    spread = jnp.where(owner_mask[..., None], block_best[:, :, None, :], very_low)
    row_best = jnp.max(spread, axis=1)
    slot_best = jnp.max(jnp.where(owner_mask[..., None], row_best[:, None, :, :], very_low), axis=2)
    slot_best = jnp.where(used_slot[..., None], slot_best, 0.0)
    weights_full = jnp.where(
        used_slot[:, :, None, None], jnp.exp(scores - slot_best[..., None]), 0.0
    )
    slot_weight = jnp.sum(weights_full, axis=3)
    slot_value = jnp.einsum(
        "hsgt,hstd->hsgd",
        weights_full.astype(jnp.bfloat16),
        value_block_store,
        preferred_element_type=jnp.float32,
    )
    row_weight = jnp.einsum(
        "hsr,hsg->rhg", owner_full, slot_weight, precision=lax.Precision.HIGHEST
    )
    row_value = jnp.einsum(
        "hsr,hsgd->rhgd", owner_full, slot_value, precision=lax.Precision.HIGHEST
    )
    row_high = jnp.transpose(row_best, (1, 0, 2))
    lenders = lax.axis_size("lender")
    home_rows = row_count // lenders
    came_best, came_weight, came_value = (
        lax.all_to_all(row_high, "lender", split_axis=0, concat_axis=0, tiled=True),
        lax.all_to_all(row_weight, "lender", split_axis=0, concat_axis=0, tiled=True),
        lax.all_to_all(row_value, "lender", split_axis=0, concat_axis=0, tiled=True),
    )
    came_best = came_best.reshape((lenders, home_rows) + came_best.shape[1:])
    came_weight = came_weight.reshape((lenders, home_rows) + came_weight.shape[1:])
    came_value = came_value.reshape((lenders, home_rows) + came_value.shape[1:])
    highest = jnp.max(came_best, axis=0)
    factor = jnp.exp(came_best - highest[None])
    home_weight = jnp.sum(came_weight * factor, axis=0)
    home_value = jnp.sum(came_value * factor[..., None], axis=0)
    home_attended = (
        (home_value / home_weight[..., None]).astype(jnp.bfloat16).reshape(home_rows, -1)
    )
    attended = lax.all_gather(home_attended, "lender", axis=0, tiled=True)
    result = lax.psum_scatter(
        jnp.dot(attended, w_out, preferred_element_type=jnp.float32),
        "tensor",
        scatter_dimension=0,
        tiled=True,
    )
    return result.astype(jnp.bfloat16)


def solution(mesh):
    in_specs = (
        P("group", "lender"),
        P("lender"),
        P("lender", "tensor"),
        P("tensor", "lender"),
        P("tensor", ("group", "lender"), None, None),
        P("tensor", ("group", "lender"), None, None),
        P("group", "tensor", None),
        P("tensor", "group"),
        P("group", "tensor"),
    )
    out_specs = P(("group", "tensor"), "lender")
    return jax.shard_map(
        per_device, mesh=mesh, in_specs=in_specs, out_specs=out_specs, check_vma=False
    )
```

profile of v0, /device:TPU:0, one launch (start us, length us, event | category | flops | bytes accessed | tf_op | source)
XLA Modules:
  0.0 116.3 jit_solution(14642296983015357791)
XLA Ops:
  6.6 0.8 convert_element_type.31
  7.4 5.2 %fusion.15 = f32[8,2048]{1,0:T(8,128)} fusion(bf16[2048,2048]{1,0:T(8,128)(2,1)} %param.11, bf16[8,2048]{1,0:T(8,128)(2,1)} %param.9, f32[2048]{0:T(1024)S(1)} %convert_element_type.31), kind=kOutput, calls=%fused_computation.26 | convolution fusion | flops 67158016 | bytes 8495104 | tf_op jit(solution)/shard_map/dot_general | solution.py:30
  13.0 2.6 %gather_fusion = s32[256]{0:T(256)S(1)} fusion(s32[8,2,128]{2,1,0:T(2,128)S(1)} %broadcast_in_dim.66, s32[256]{0:T(256)S(1)} %reshape.57), kind=kCustom, calls=%fused_computation | custom fusion | bytes 5120 | tf_op jit(solution)/shard_map/jit(take_along_axis)/gather | solution.py:39
  15.8 13.5 %psum.15 = f32[8]{0:T(128)S(1)} all-reduce(f32[8]{0:T(128)S(1)} %fusion.13), channel_id=1, replica_groups=mesh['group'=2,'lender'=4,'tensor'=4] {'lender'}, use_global_device_ids=true, to_apply=%region_4.5 | all-reduce | flops 8 | bytes 64 | tf_op jit(solution)/shard_map/psum | solution.py:31
  29.5 0.6 dynamic-slice
  30.8 19.1 %all-reduce.3.cloned.1.call-done = f32[8,2048]{1,0:T(8,128)} async-done(((f32[8,2048]{1,0:T(8,128)}), f32[8,2048]{1,0:T(8,128)}) %all-reduce.3.cloned.1.call-update) | async-done | bytes 65552 | tf_op jit(solution)/shard_map/psum | solution.py:31
  49.9 0.9 multiply_convert_fusion
  50.8 0.2 convolution_convert_fusion
  51.1 1.3 %fusion.22 = (f32[2,32,8]{2,1,0:T(8,128)S(1)}, f32[2,32,8,128]{3,2,1,0:T(8,128)S(1)}) fusion(bf16[2,32,128,128]{3,2,1,0:T(8,128)(2,1)S(1)} %copy-done, bf16[2,32,8,128]{3,1,2,0:T(8,128)(2,1)S(1)} %convolution_convert_fusion), kind=kOutput, calls=%fused_computation.43 | convolution fusion | flops 16842240 | bytes 2492416 | tf_op jit(solution)/shard_map/hsgd,hstd->hsgt/dot_general | solution.py:53
  52.7 0.6 copy.57
  53.3 3.4 %all-to-all-start.1 = ((f32[8,2,8]{2,1,0:T(2,128)}), f32[8,2,8]{2,1,0:T(2,128)S(1)}, u32[]{:S(2)}, u32[]{:S(2)}) async-start(f32[8,2,8]{2,1,0:T(2,128)} %copy.57), calls=%async_computation.1 | async-start | bytes 16384 | tf_op jit(solution)/shard_map/all_to_all | solution.py:79
  56.7 0.3 fusion.1
  57.0 2.3 %fusion.3 = f32[2,32,8,128]{3,2,1,0:T(8,128)S(1)} fusion(bf16[2,32,128,128]{3,2,1,0:T(8,128)(2,1)} %param.14, f32[2,32,8,128]{3,2,1,0:T(8,128)S(1)} %get-tuple-element.8, f32[2,32,8]{2,1,0:T(8,128)S(1)} %copy.53, pred[2,32]{1,0:T(4,128)(4,1)S(1)} %bitcast_reduce_fusion), kind=kOutput, calls=%fused_computation.8 | convolution fusion | flops 16973824 | bytes 2623552 | tf_op jit(solution)/shard_map/hsgt,hstd->hsgd/dot_general | solution.py:63
  59.5 0.7 copy.63
  60.2 2.1 %all-to-all-done.1 = f32[8,2,8]{2,1,0:T(2,128)S(1)} async-done(((f32[8,2,8]{2,1,0:T(2,128)}), f32[8,2,8]{2,1,0:T(2,128)S(1)}, u32[]{:S(2)}, u32[]{:S(2)}) %all-to-all-start.1) | async-done | bytes 544 | tf_op jit(solution)/shard_map/all_to_all | solution.py:79
  62.3 3.2 %all-to-all-start.2 = ((f32[8,2,8]{2,1,0:T(2,128)}), f32[8,2,8]{2,1,0:T(2,128)S(1)}, u32[]{:S(2)}, u32[]{:S(2)}) async-start(f32[8,2,8]{2,1,0:T(2,128)} %copy.63), calls=%async_computation.2 | async-start | bytes 16384 | tf_op jit(solution)/shard_map/all_to_all | solution.py:80
  65.8 0.6 copy.56
  66.4 4.7 %all-to-all-done.2 = f32[8,2,8]{2,1,0:T(2,128)S(1)} async-done(((f32[8,2,8]{2,1,0:T(2,128)}), f32[8,2,8]{2,1,0:T(2,128)S(1)}, u32[]{:S(2)}, u32[]{:S(2)}) %all-to-all-start.2) | async-done | bytes 544 | tf_op jit(solution)/shard_map/all_to_all | solution.py:80
  71.1 3.3 %all-to-all-start = ((f32[8,2,8,128]{3,2,1,0:T(8,128)}), f32[8,2,8,128]{3,2,1,0:T(8,128)S(1)}, u32[]{:S(2)}, u32[]{:S(2)}) async-start(f32[8,2,8,128]{3,2,1,0:T(8,128)} %copy.56), calls=%async_computation | async-start | bytes 131072 | tf_op jit(solution)/shard_map/all_to_all | solution.py:81
  74.6 5.5 %all-to-all-done = f32[8,2,8,128]{3,2,1,0:T(8,128)S(1)} async-done(((f32[8,2,8,128]{3,2,1,0:T(8,128)}), f32[8,2,8,128]{3,2,1,0:T(8,128)S(1)}, u32[]{:S(2)}, u32[]{:S(2)}) %all-to-all-start) | async-done | bytes 65568 | tf_op jit(solution)/shard_map/all_to_all | solution.py:81
  80.4 13.1 %all-gather = bf16[4,2,2048]{2,1,0:T(2,128)(2,1)S(1)} all-gather(bf16[1,2,2048]{2,1,0:T(2,128)(2,1)S(1)} %bitcast.37), channel_id=1, replica_groups=mesh['group'=2,'lender'=4,'tensor'=4] {'lender'}, dimensions={0}, use_global_device_ids=true | all-gather | bytes 40960 | tf_op jit(solution)/shard_map/all_gather | solution.py:93
  93.6 4.6 %fusion.23 = f32[8,2048]{1,0:T(8,128)S(1)} fusion(bf16[8,2048]{1,0:T(8,128)(2,1)S(1)} %reshape.69, bf16[2048,2048]{1,0:T(8,128)(2,1)} %param.12), kind=kOutput, calls=%fused_computation.44 | convolution fusion | flops 67108864 | bytes 8486912 | tf_op jit(solution)/shard_map/dot_general | solution.py:95
  98.2 10.7 %all-reduce = bf16[8,2048]{1,0:T(8,128)(2,1)S(1)} all-reduce(f32[8,2048]{1,0:T(8,128)S(1)} %fusion.23), channel_id=2, replica_groups=mesh['group'=2,'lender'=4,'tensor'=4] {'tensor'}, use_global_device_ids=true, to_apply=%region_12.13.clone | all-reduce | flops 16384 | bytes 98304
  108.8 0.6 dynamic-slice_convert_fusion
  (42 shorter events, 2.1 us)
Async XLA Ops:
  6.5 44.5 %copy-start = (bf16[2,32,128,128]{3,2,1,0:T(8,128)(2,1)S(1)}, bf16[2,32,128,128]{3,2,1,0:T(8,128)(2,1)}, u32[]{:S(2)}) copy-start(bf16[2,32,128,128]{3,2,1,0:T(8,128)(2,1)} %param.13) | copy-start | bytes 6291460
  6.5 6.2 %copy-start.1 = (bf16[8,2048]{1,0:T(8,128)(2,1)S(1)}, bf16[8,2048]{1,0:T(8,128)(2,1)}, u32[]{:S(2)}) copy-start(bf16[8,2048]{1,0:T(8,128)(2,1)} %param.9) | copy-start | bytes 98308
  6.5 6.3 %copy-start.2 = (s32[8,2,16]{2,1,0:T(2,128)S(1)}, s32[8,2,16]{2,1,0:T(2,128)}, u32[]{:S(2)}) copy-start(s32[8,2,16]{2,1,0:T(2,128)} %param.15) | copy-start | bytes 3076
  6.5 6.4 %copy-start.3 = (s32[2,128]{1,0:T(2,128)S(1)}, s32[2,128]{1,0:T(2,128)}, u32[]{:S(2)}) copy-start(s32[2,128]{1,0:T(2,128)} %param.16) | copy-start | bytes 3076
  6.5 43.4 %all-reduce.3.cloned.1.call-start = ((), (), s32[]{:S(2)}) async-start(), calls=%async_computation.3 | async-start | bytes 131072 | tf_op jit(solution)/shard_map/psum | solution.py:31
  7.4 8.2 %copy-start.4 = (s32[8,2]{0,1:T(2,128)S(1)}, s32[8,2]{0,1:T(2,128)}, u32[]{:S(2)}) copy-start(s32[8,2]{0,1:T(2,128)} %param.17) | copy-start | bytes 196
  7.4 22.1 %copy-start.5 = (u32[32]{0:T(128)S(1)}, u32[32]{0:T(128)}, u32[]{:S(2)}) copy-start(u32[32]{0:T(128)} %constant.64) | copy-start | bytes 388
  53.3 9.0 %all-to-all-start.1 = ((f32[8,2,8]{2,1,0:T(2,128)}), f32[8,2,8]{2,1,0:T(2,128)S(1)}, u32[]{:S(2)}, u32[]{:S(2)}) async-start(f32[8,2,8]{2,1,0:T(2,128)} %copy.57), calls=%async_computation.1 | async-start | bytes 16384 | tf_op jit(solution)/shard_map/all_to_all | solution.py:79
  62.3 8.8 %all-to-all-start.2 = ((f32[8,2,8]{2,1,0:T(2,128)}), f32[8,2,8]{2,1,0:T(2,128)S(1)}, u32[]{:S(2)}, u32[]{:S(2)}) async-start(f32[8,2,8]{2,1,0:T(2,128)} %copy.63), calls=%async_computation.2 | async-start | bytes 16384 | tf_op jit(solution)/shard_map/all_to_all | solution.py:80
  71.1 9.1 %all-to-all-start = ((f32[8,2,8,128]{3,2,1,0:T(8,128)}), f32[8,2,8,128]{3,2,1,0:T(8,128)S(1)}, u32[]{:S(2)}, u32[]{:S(2)}) async-start(f32[8,2,8,128]{3,2,1,0:T(8,128)} %copy.56), calls=%async_computation | async-start | bytes 131072 | tf_op jit(solution)/shard_map/all_to_all | solution.py:81
Sparse Core Ops, SparseCore 0:
  12.8 37.0 all-reduce.2
where the time goes:
time: 117 us; the launch traced here: 116 us
  blocking collectives  37.3 us (32%)
  waiting for transfers between devices  31.5 us (27%)
  between operations  14.2 us (12%)
  matrix products  14 us (12%)
  starting transfers between devices  9.94 us (8%)
  local copies, waits for them, and re-layouts  6.38 us (5%)
  other arithmetic  2.96 us (3%)
    psum x1, waiting for transfers between devices, per_device(): projected, square_sum = lax.psum((partial_value, squares), 'lender')  19.1 us
    psum x1, blocking collectives, per_device(): projected, square_sum = lax.psum((partial_value, squares), 'lender')  13.5 us
    all_gather x1, blocking collectives, per_device(): attended = lax.all_gather(home_attended, 'lender', axis=0, tiled=True)  13.1 us
    unnamed x1, blocking collectives  10.7 us
    all_to_all x1, waiting for transfers between devices, per_device(): lax.all_to_all(row_value, 'lender', split_axis=0, concat_axis=0, tiled=True)  5.54 us
    dot_general x1, matrix products, per_device(): partial_value = jnp.dot(scaled, w_query, preferred_element_type=jnp.float32)  5.24 us
    all_to_all x1, waiting for transfers between devices, per_device(): lax.all_to_all(row_weight, 'lender', split_axis=0, concat_axis=0, tiled=T...  4.68 us
    dot_general x1, matrix products, per_device(): jnp.dot(attended, w_out, preferred_element_type=jnp.float32)  4.57 us
  transfers between devices with their start and end apart: 4, of which 4 were waited for; matrix products, arithmetic and copies ran while one was open for 7% of the time, Pallas kernels for 0%

commit v1 on v0

--- a/solution.py
+++ b/solution.py
@@ -6,6 +6,18 @@
 D = 8192
 very_low = -1e30
 epsilon = 1e-05
+
+
+def collect(shard, axis, dim):
+    ways, here = (lax.axis_size(axis), lax.axis_index(axis))
+    grown, reach = (shard, 1)
+    while reach < ways:
+        theirs = lax.ppermute(grown, axis, [(d, d ^ reach) for d in range(ways)])
+        mine_first = jnp.concatenate([grown, theirs], axis=dim)
+        theirs_first = jnp.concatenate([theirs, grown], axis=dim)
+        grown = jnp.where(here & reach == 0, mine_first, theirs_first)
+        reach = 2 * reach
+    return grown
 
 
 def per_device(
@@ -90,7 +102,7 @@
     home_attended = (
         (home_value / home_weight[..., None]).astype(jnp.bfloat16).reshape(home_rows, -1)
     )
-    attended = lax.all_gather(home_attended, "lender", axis=0, tiled=True)
+    attended = collect(home_attended, "lender", 0)
     result = lax.psum_scatter(
         jnp.dot(attended, w_out, preferred_element_type=jnp.float32),
         "tensor",

time: 117 us -> 112 us (0.957)
  blocking collectives: 37.3 us -> 24.1 us
  waiting for transfers between devices: 31.5 us -> 38 us
  starting transfers between devices: 9.94 us -> 11.7 us
    all_gather x1 -> x0, blocking collectives: 13.1 us -> none  [per_device(): attended = lax.all_gather(home_attended, 'lender', axis=0, tiled=True)]
    ppermute x0 -> x2, waiting for transfers between devices: none -> 5.4 us  [collect(): theirs = lax.ppermute(grown, axis, [(d, d ^ reach) for d in range(ways)])]
    ppermute x0 -> x2, starting transfers between devices: none -> 1.78 us  [collect(): theirs = lax.ppermute(grown, axis, [(d, d ^ reach) for d in range(ways)])]
    psum x1, waiting for transfers between devices: 19.1 us -> 20.3 us  [per_device(): projected, square_sum = lax.psum((partial_value, squares), 'lender')]
  transfers between devices with their start and end apart: 4 -> 6, of which waited for: 4 -> 6; matrix products, arithmetic and copies ran while one was open for 7% -> 8% of each run, Pallas kernels for 0% -> 0%
where the time goes in v1:
time: 112 us; the launch traced here: 111 us
  waiting for transfers between devices  38 us (34%)
  blocking collectives  24.1 us (22%)
  between operations  14.2 us (13%)
  matrix products  14 us (12%)
  starting transfers between devices  11.7 us (10%)
  local copies, waits for them, and re-layouts  6.36 us (6%)
  other arithmetic  2.99 us (3%)
    psum x1, waiting for transfers between devices, per_device(): projected, square_sum = lax.psum((partial_value, squares), 'lender')  20.3 us
    psum x1, blocking collectives, per_device(): projected, square_sum = lax.psum((partial_value, squares), 'lender')  13.5 us
    unnamed x1, blocking collectives  10.7 us
    all_to_all x1, waiting for transfers between devices, per_device(): lax.all_to_all(row_value, 'lender', split_axis=0, concat_axis=0, tiled=True)  5.46 us
    ppermute x2, waiting for transfers between devices, collect(): theirs = lax.ppermute(grown, axis, [(d, d ^ reach) for d in range(ways)])  5.4 us
    dot_general x1, matrix products, per_device(): partial_value = jnp.dot(scaled, w_query, preferred_element_type=jnp.float32)  5.21 us
    all_to_all x1, waiting for transfers between devices, per_device(): lax.all_to_all(row_weight, 'lender', split_axis=0, concat_axis=0, tiled=T...  4.68 us
    dot_general x1, matrix products, per_device(): jnp.dot(attended, w_out, preferred_element_type=jnp.float32)  4.57 us
  transfers between devices with their start and end apart: 6, of which 6 were waited for; matrix products, arithmetic and copies ran while one was open for 8% of the time, Pallas kernels for 0%

profile of v1, /device:TPU:0, one launch (start us, length us, event | category | flops | bytes accessed | tf_op | source)
XLA Modules:
  0.0 111.4 jit_solution(6589503035312834621)
XLA Ops:
  6.6 0.8 convert_element_type.31
  7.4 5.2 %fusion.15 = f32[8,2048]{1,0:T(8,128)} fusion(bf16[2048,2048]{1,0:T(8,128)(2,1)} %param.11, bf16[8,2048]{1,0:T(8,128)(2,1)} %param.9, f32[2048]{0:T(1024)S(1)} %convert_element_type.31), kind=kOutput, calls=%fused_computation.26 | convolution fusion | flops 67158016 | bytes 8495104 | tf_op jit(solution)/shard_map/dot_general | solution.py:42
  13.1 2.6 %gather_fusion = s32[256]{0:T(256)S(1)} fusion(s32[8,2,128]{2,1,0:T(2,128)S(1)} %broadcast_in_dim.66, s32[256]{0:T(256)S(1)} %reshape.57), kind=kCustom, calls=%fused_computation | custom fusion | bytes 5120 | tf_op jit(solution)/shard_map/jit(take_along_axis)/gather | solution.py:51
  15.8 13.5 %psum.15 = f32[8]{0:T(128)S(1)} all-reduce(f32[8]{0:T(128)S(1)} %fusion.13), channel_id=1, replica_groups=mesh['group'=2,'lender'=4,'tensor'=4] {'lender'}, use_global_device_ids=true, to_apply=%region_4.5 | all-reduce | flops 8 | bytes 64 | tf_op jit(solution)/shard_map/psum | solution.py:43
  29.5 20.3 %all-reduce.3.cloned.1.call-done = f32[8,2048]{1,0:T(8,128)} async-done(((f32[8,2048]{1,0:T(8,128)}), f32[8,2048]{1,0:T(8,128)}) %all-reduce.3.cloned.1.call-update) | async-done | bytes 65552 | tf_op jit(solution)/shard_map/psum | solution.py:43
  49.9 0.9 multiply_convert_fusion
  51.0 1.3 %fusion.30 = (f32[2,32,8]{2,1,0:T(8,128)S(1)}, f32[2,32,8,128]{3,2,1,0:T(8,128)S(1)}) fusion(bf16[2,32,128,128]{3,2,1,0:T(8,128)(2,1)S(1)} %copy-done, bf16[2,32,8,128]{3,1,2,0:T(8,128)(2,1)S(1)} %convolution_convert_fusion), kind=kOutput, calls=%fused_computation.53 | convolution fusion | flops 16842240 | bytes 2492416 | tf_op jit(solution)/shard_map/hsgd,hstd->hsgt/dot_general | solution.py:65
  52.7 0.6 copy.57
  53.3 3.4 %all-to-all-start.1 = ((f32[8,2,8]{2,1,0:T(2,128)}), f32[8,2,8]{2,1,0:T(2,128)S(1)}, u32[]{:S(2)}, u32[]{:S(2)}) async-start(f32[8,2,8]{2,1,0:T(2,128)} %copy.57), calls=%async_computation.1 | async-start | bytes 16384 | tf_op jit(solution)/shard_map/all_to_all | solution.py:91
  57.0 2.3 %fusion.3 = f32[2,32,8,128]{3,2,1,0:T(8,128)S(1)} fusion(bf16[2,32,128,128]{3,2,1,0:T(8,128)(2,1)} %param.14, f32[2,32,8,128]{3,2,1,0:T(8,128)S(1)} %get-tuple-element.8, f32[2,32,8]{2,1,0:T(8,128)S(1)} %copy.53, pred[2,32]{1,0:T(4,128)(4,1)S(1)} %bitcast_reduce_fusion), kind=kOutput, calls=%fused_computation.8 | convolution fusion | flops 16973824 | bytes 2623552 | tf_op jit(solution)/shard_map/hsgt,hstd->hsgd/dot_general | solution.py:75
  59.5 0.7 copy.63
  60.1 2.1 %all-to-all-done.1 = f32[8,2,8]{2,1,0:T(2,128)S(1)} async-done(((f32[8,2,8]{2,1,0:T(2,128)}), f32[8,2,8]{2,1,0:T(2,128)S(1)}, u32[]{:S(2)}, u32[]{:S(2)}) %all-to-all-start.1) | async-done | bytes 544 | tf_op jit(solution)/shard_map/all_to_all | solution.py:91
  62.2 3.2 %all-to-all-start.2 = ((f32[8,2,8]{2,1,0:T(2,128)}), f32[8,2,8]{2,1,0:T(2,128)S(1)}, u32[]{:S(2)}, u32[]{:S(2)}) async-start(f32[8,2,8]{2,1,0:T(2,128)} %copy.63), calls=%async_computation.2 | async-start | bytes 16384 | tf_op jit(solution)/shard_map/all_to_all | solution.py:92
  65.7 0.6 copy.56
  66.4 4.7 %all-to-all-done.2 = f32[8,2,8]{2,1,0:T(2,128)S(1)} async-done(((f32[8,2,8]{2,1,0:T(2,128)}), f32[8,2,8]{2,1,0:T(2,128)S(1)}, u32[]{:S(2)}, u32[]{:S(2)}) %all-to-all-start.2) | async-done | bytes 544 | tf_op jit(solution)/shard_map/all_to_all | solution.py:92
  71.0 3.3 %all-to-all-start = ((f32[8,2,8,128]{3,2,1,0:T(8,128)}), f32[8,2,8,128]{3,2,1,0:T(8,128)S(1)}, u32[]{:S(2)}, u32[]{:S(2)}) async-start(f32[8,2,8,128]{3,2,1,0:T(8,128)} %copy.56), calls=%async_computation | async-start | bytes 131072 | tf_op jit(solution)/shard_map/all_to_all | solution.py:93
  74.6 5.5 %all-to-all-done = f32[8,2,8,128]{3,2,1,0:T(8,128)S(1)} async-done(((f32[8,2,8,128]{3,2,1,0:T(8,128)}), f32[8,2,8,128]{3,2,1,0:T(8,128)S(1)}, u32[]{:S(2)}, u32[]{:S(2)}) %all-to-all-start) | async-done | bytes 65568 | tf_op jit(solution)/shard_map/all_to_all | solution.py:93
  80.3 1.0 collective-permute-start
  81.3 2.7 %collective-permute-done = bf16[2,2048]{1,0:T(2,128)(2,1)S(1)} collective-permute-done((bf16[2,2048]{1,0:T(2,128)(2,1)S(1)}, bf16[2,2048]{1,0:T(2,128)(2,1)S(1)}, u32[]{:S(2)}, u32[]{:S(2)}) %collective-permute-start) | collective-permute-done | bytes 8224 | tf_op jit(solution)/shard_map/ppermute | solution.py:15
  84.0 0.8 collective-permute-start.1
  86.1 2.7 %collective-permute-done.1 = bf16[4,2048]{1,0:T(4,128)(2,1)S(1)} collective-permute-done((bf16[4,2048]{1,0:T(4,128)(2,1)S(1)}, bf16[4,2048]{1,0:T(4,128)(2,1)S(1)}, u32[]{:S(2)}, u32[]{:S(2)}) %collective-permute-start.1) | collective-permute-done | bytes 16416 | tf_op jit(solution)/shard_map/ppermute | solution.py:15
  88.8 4.6 %fusion.17 = f32[8,2048]{1,0:T(8,128)S(1)} fusion(bf16[2048,2048]{1,0:T(8,128)(2,1)} %param.12, bf16[4,2048]{1,0:T(4,128)(2,1)S(1)} %collective-permute-done.1, bf16[4,2048]{1,0:T(4,128)(2,1)S(1)} %maximum_select_fusion.2, pred[]{:T(512)S(6)} %eq.19), kind=kOutput, calls=%fused_computation.28 | convolution fusion | flops 67256320 | bytes 8486913 | tf_op jit(solution)/shard_map/dot_general | solution.py:107
  93.3 10.7 %all-reduce = bf16[8,2048]{1,0:T(8,128)(2,1)S(1)} all-reduce(f32[8,2048]{1,0:T(8,128)S(1)} %fusion.17), channel_id=2, replica_groups=mesh['group'=2,'lender'=4,'tensor'=4] {'tensor'}, use_global_device_ids=true, to_apply=%region_12.13.clone | all-reduce | flops 16384 | bytes 98304
  104.0 0.6 dynamic-slice_convert_fusion
  (45 shorter events, 3.2 us)
Async XLA Ops:
  6.5 44.5 %copy-start = (bf16[2,32,128,128]{3,2,1,0:T(8,128)(2,1)S(1)}, bf16[2,32,128,128]{3,2,1,0:T(8,128)(2,1)}, u32[]{:S(2)}) copy-start(bf16[2,32,128,128]{3,2,1,0:T(8,128)(2,1)} %param.13) | copy-start | bytes 6291460
  6.5 6.1 %copy-start.1 = (bf16[8,2048]{1,0:T(8,128)(2,1)S(1)}, bf16[8,2048]{1,0:T(8,128)(2,1)}, u32[]{:S(2)}) copy-start(bf16[8,2048]{1,0:T(8,128)(2,1)} %param.9) | copy-start | bytes 98308
  6.5 6.3 %copy-start.2 = (s32[8,2,16]{2,1,0:T(2,128)S(1)}, s32[8,2,16]{2,1,0:T(2,128)}, u32[]{:S(2)}) copy-start(s32[8,2,16]{2,1,0:T(2,128)} %param.15) | copy-start | bytes 3076
  6.5 6.4 %copy-start.3 = (s32[8,2]{0,1:T(2,128)S(1)}, s32[8,2]{0,1:T(2,128)}, u32[]{:S(2)}) copy-start(s32[8,2]{0,1:T(2,128)} %param.17) | copy-start | bytes 196
  6.5 6.5 %copy-start.4 = (s32[2,128]{1,0:T(2,128)S(1)}, s32[2,128]{1,0:T(2,128)}, u32[]{:S(2)}) copy-start(s32[2,128]{1,0:T(2,128)} %param.16) | copy-start | bytes 3076
  6.5 43.3 %all-reduce.3.cloned.1.call-start = ((), (), s32[]{:S(2)}) async-start(), calls=%async_computation.3 | async-start | bytes 131072 | tf_op jit(solution)/shard_map/psum | solution.py:43
  12.6 72.2 %copy-start.5 = (u32[32]{0:T(128)S(1)}, u32[32]{0:T(128)}, u32[]{:S(2)}) copy-start(u32[32]{0:T(128)} %constant.69) | copy-start | bytes 388
  53.3 9.0 %all-to-all-start.1 = ((f32[8,2,8]{2,1,0:T(2,128)}), f32[8,2,8]{2,1,0:T(2,128)S(1)}, u32[]{:S(2)}, u32[]{:S(2)}) async-start(f32[8,2,8]{2,1,0:T(2,128)} %copy.57), calls=%async_computation.1 | async-start | bytes 16384 | tf_op jit(solution)/shard_map/all_to_all | solution.py:91
  62.2 8.8 %all-to-all-start.2 = ((f32[8,2,8]{2,1,0:T(2,128)}), f32[8,2,8]{2,1,0:T(2,128)S(1)}, u32[]{:S(2)}, u32[]{:S(2)}) async-start(f32[8,2,8]{2,1,0:T(2,128)} %copy.63), calls=%async_computation.2 | async-start | bytes 16384 | tf_op jit(solution)/shard_map/all_to_all | solution.py:92
  71.0 9.0 %all-to-all-start = ((f32[8,2,8,128]{3,2,1,0:T(8,128)}), f32[8,2,8,128]{3,2,1,0:T(8,128)S(1)}, u32[]{:S(2)}, u32[]{:S(2)}) async-start(f32[8,2,8,128]{3,2,1,0:T(8,128)} %copy.56), calls=%async_computation | async-start | bytes 131072 | tf_op jit(solution)/shard_map/all_to_all | solution.py:93
  80.3 3.7 %collective-permute-start = (bf16[2,2048]{1,0:T(2,128)(2,1)S(1)}, bf16[2,2048]{1,0:T(2,128)(2,1)S(1)}, u32[]{:S(2)}, u32[]{:S(2)}) collective-permute-start(bf16[2,2048]{1,0:T(2,128)(2,1)S(1)} %bitcast.36), channel_id=1, source_target_pairs={{0,4},{4,0},{8,12},{12,8},{1,5},{5,1},{9,13},{13,9},{2,6},{6,2},{1... | collective-permute-start | bytes 24584 | tf_op jit(solution)/shard_map/ppermute | solution.py:15
  84.0 4.7 %collective-permute-start.1 = (bf16[4,2048]{1,0:T(4,128)(2,1)S(1)}, bf16[4,2048]{1,0:T(4,128)(2,1)S(1)}, u32[]{:S(2)}, u32[]{:S(2)}) collective-permute-start(bf16[4,2048]{1,0:T(4,128)(2,1)S(1)} %maximum_select_fusion.2), channel_id=1, source_target_pairs={{0,8},{4,12},{8,0},{12,4},{1,9},{5,13},{9,1},{13,5},{2,10},{6,14},... | collective-permute-start | bytes 49160 | tf_op jit(solution)/shard_map/ppermute | solution.py:15
Sparse Core Ops, SparseCore 0:
  12.8 37.0 all-reduce.2
